TPU v7x, 32 devices: a whole 2x2x4 slice. The times are simulated.
32 devices in a mesh: ri: 8 (over z, core), rj: 4 (over y, x).
Axes of the slice: x: 2, y: 2, z: 4, core: 2. Of those that a mesh axis runs over, the one named last changes fastest.
Arguments:
- pair: bfloat16 [320, 320, 128], P('ri', 'rj'), may hold values from -6 to 6
- in_gain: float32 [128], replicated, may hold values from 0.1 to 1.9
- in_bias: float32 [128], replicated, may hold values from -3 to 3
- w_in: bfloat16 [128, 512], replicated, may hold values from -0.5 to 0.5
- w_gate: bfloat16 [128, 128], replicated, may hold values from -0.5 to 0.5
- out_gain: float32 [128], replicated, may hold values from 0.1 to 1.9
- out_bias: float32 [128], replicated, may hold values from -3 to 3
- w_out: bfloat16 [128, 128], replicated, may hold values from -0.5 to 0.5
Outputs:
- update: bfloat16 [320, 320, 128], P('ri', 'rj')
All inputs are finite; a program needn't handle non-finite values.
Results may differ from a plain program's by a relative error of at most 0.015.
Values may be sent and summed in bfloat16 or wider, within the bound.
A program may use at most 128 MiB of HBM per device.

v0:
```python
import jax
import jax.numpy as jnp
from jax import lax
from jax.sharding import PartitionSpec as P


def layer_norm(values, gain, bias):
    mean = jnp.mean(values, axis=-1, keepdims=True)
    centered = values - mean
    var = jnp.mean(centered * centered, axis=-1, keepdims=True)
    return centered * lax.rsqrt(var + 1e-05) * gain + bias


def local(pair, in_gain, in_bias, w_in, w_gate, out_gain, out_bias, w_out):
    rows, cols, chans = pair.shape
    hidden = w_out.shape[0]
    normed = layer_norm(pair.astype(jnp.float32), in_gain, in_bias).astype(jnp.bfloat16)
    flat = normed.reshape(rows * cols, chans)
    proj = jnp.dot(flat, w_in, preferred_element_type=jnp.float32)
    a_tile = (
        (jax.nn.sigmoid(proj[:, hidden : 2 * hidden]) * proj[:, :hidden])
        .astype(jnp.bfloat16)
        .reshape(rows, cols, hidden)
    )
    b_tile = (
        (jax.nn.sigmoid(proj[:, 3 * hidden :]) * proj[:, 2 * hidden : 3 * hidden])
        .astype(jnp.bfloat16)
        .reshape(rows, cols, hidden)
    )
    gate = jax.nn.sigmoid(jnp.dot(flat, w_gate, preferred_element_type=jnp.float32)).astype(
        jnp.bfloat16
    )
    a_rows = lax.all_gather(a_tile, "rj", axis=1, tiled=True)
    product = lax.dot_general(
        a_rows, b_tile, (((0,), (0,)), ((2,), (2,))), preferred_element_type=jnp.float32
    )
    summed = lax.psum_scatter(
        jnp.transpose(product, (1, 2, 0)).astype(jnp.bfloat16),
        "ri",
        scatter_dimension=0,
        tiled=True,
    ).astype(jnp.float32)
    tri = summed.reshape(rows * cols, hidden)
    tri_normed = layer_norm(tri, out_gain, out_bias).astype(jnp.bfloat16)
    mixed = jnp.dot(tri_normed, w_out, preferred_element_type=jnp.float32)
    update = gate.astype(jnp.float32) * mixed
    return update.reshape(rows, cols, chans).astype(jnp.bfloat16)


def solution(mesh):
    return jax.shard_map(
        local,
        mesh=mesh,
        in_specs=(P("ri", "rj", None), P(), P(), P(), P(), P(), P(), P()),
        out_specs=P("ri", "rj", None),
        check_vma=False,
    )
```

profile of v0, /device:TPU:0, one launch (start us, length us, event | category | flops | bytes accessed | tf_op | source)
XLA Modules:
  0.0 174.6 jit_solution(12855295967835624654)
XLA Ops:
  6.5 0.0 copy-start
  6.5 0.0 all-gather.2.cloned.1.call-start
  6.6 1.6 convert_reduce_fusion
  8.2 2.3 %fusion.8 = f32[40,80]{1,0:T(8,128)S(1)} fusion(bf16[40,80,128]{2,1,0:T(8,128)(2,1)} %param.8, f32[40,80]{1,0:T(8,128)S(1)} %broadcast_multiply_fusion.1), kind=kLoop, calls=%fused_computation.13 | loop fusion | flops 1635200 | bytes 844800 | tf_op jit(solution)/shard_map/reduce_sum | solution.py:10
  10.6 0.0 copy-done.1
  10.6 0.0 copy-done.4
  10.6 0.0 copy-done.5
  10.6 1.1 fusion.11
  11.7 1.0 fusion.24
  12.7 0.9 fusion.12
  13.6 1.1 copy.28
  14.7 0.0 all-gather.2.cloned.1.call-update
  14.7 0.0 reduce-scatter.2.cloned.1.call-start
  14.8 1.6 copy.30
  16.4 46.1 %all-gather.2.cloned.1.call-done = bf16[40,320,128]{2,0,1:T(8,128)(2,1)} async-done(((bf16[40,80,128]{2,0,1:T(8,128)(2,1)}), bf16[40,320,128]{2,0,1:T(8,128)(2,1)}) %all-gather.2.cloned.1.call-update) | async-done | bytes 3276816 | tf_op jit(solution)/shard_map/all_gather | solution.py:33
  62.5 6.7 %copy.29 = bf16[40,320,128]{1,0,2:T(8,128)(2,1)} copy(bf16[40,320,128]{2,0,1:T(8,128)(2,1)} %all-gather.2.cloned.1.call-done) | data formatting | bytes 6553600 | tf_op jit(solution)/shard_map/all_gather | solution.py:33
  69.3 7.4 %convert_bitcast_fusion = bf16[320,80,128]{0,1,2:T(8,128)(2,1)} fusion(bf16[40,320,128]{1,0,2:T(8,128)(2,1)} %copy.29, bf16[40,80,128]{1,0,2:T(8,128)(2,1)S(1)} %copy.30), kind=kOutput, calls=%fused_computation | convolution fusion | flops 265420800 | bytes 10649600 | tf_op jit(solution)/shard_map/dot_general | solution.py:34
  76.7 11.5 %copy.31 = bf16[320,80,128]{2,1,0:T(8,128)(2,1)} copy(bf16[320,80,128]{0,1,2:T(8,128)(2,1)} %convert_bitcast_fusion) | data formatting | bytes 13107200 | tf_op jit(solution)/shard_map/convert_element_type | solution.py:38
  88.2 0.0 reduce-scatter.2.cloned.1.call-update
  88.2 0.7 copy-done.8
  89.0 0.6 fusion.4
  89.5 0.0 copy-start.6
  89.6 0.0 copy-start.7
  89.6 0.0 copy-start.3
  89.6 71.0 %reduce-scatter.2.cloned.1.call-done = bf16[40,80,128]{2,1,0:T(8,128)(2,1)} async-done(((bf16[320,80,128]{2,1,0:T(8,128)(2,1)}), bf16[40,80,128]{2,1,0:T(8,128)(2,1)}) %reduce-scatter.2.cloned.1.call-update) | async-done | bytes 819216 | tf_op jit(solution)/shard_map/reduce_scatter | solution.py:37
  160.6 1.6 convert_reduce_fusion.1
  162.2 0.1 div.29
  162.3 2.3 %multiply_reduce_fusion = f32[40,80]{1,0:T(8,128)S(1)} fusion(f32[40,80]{1,0:T(8,128)S(1)} %broadcast_multiply_fusion, bf16[40,80,128]{2,1,0:T(8,128)(2,1)} %reduce-scatter.2.cloned.1.call-done), kind=kLoop, calls=%fused_computation.34 | loop fusion | flops 1635200 | bytes 844800 | tf_op jit(solution)/shard_map/reduce_sum | solution.py:10
  164.7 0.1 rsqrt.21
  164.8 1.7 %fusion.23 = bf16[3200,128]{1,0:T(8,128)(2,1)S(1)} fusion(f32[128]{0:T(128)S(1)} %copy-done.6, f32[128]{0:T(128)S(1)} %copy-done.7, f32[3200]{0:T(1024)S(1)} %rsqrt.21, f32[3200]{0:T(1024)S(1)} %div.29, bf16[40,80,128]{2,1,0:T(8,128)(2,1)S(1)} %copy-done.2), kind=kLoop, calls=%fused_computation.33 | loop fusion | flops 2457600 | bytes 1665024 | tf_op jit(solution)/shard_map/convert_element_type | solution.py:44
  166.5 0.0 copy-done.3
  166.5 1.2 fusion.5
  (13 shorter events, 0.0 us)
Async XLA Ops:
  6.5 5.2 %copy-start = (bf16[128,512]{1,0:T(8,128)(2,1)S(1)}, bf16[128,512]{1,0:T(8,128)(2,1)}, u32[]{:S(2)}) copy-start(bf16[128,512]{1,0:T(8,128)(2,1)} %param.11) | copy-start | bytes 393220
  6.5 4.1 %copy-start.1 = (bf16[40,80,128]{2,1,0:T(8,128)(2,1)S(1)}, bf16[40,80,128]{2,1,0:T(8,128)(2,1)}, u32[]{:S(2)}) copy-start(bf16[40,80,128]{2,1,0:T(8,128)(2,1)} %param.8) | copy-start | bytes 2457604
  6.5 4.1 %copy-start.4 = (f32[128]{0:T(128)S(1)}, f32[128]{0:T(128)}, u32[]{:S(2)}) copy-start(f32[128]{0:T(128)} %param.10) | copy-start | bytes 1540
  6.5 4.1 %copy-start.5 = (f32[128]{0:T(128)S(1)}, f32[128]{0:T(128)}, u32[]{:S(2)}) copy-start(f32[128]{0:T(128)} %param.9) | copy-start | bytes 1540
  6.5 56.0 %all-gather.2.cloned.1.call-start = ((), (), s32[]{:S(2)}) async-start(), calls=%async_computation.1 | async-start | bytes 4096000 | tf_op jit(solution)/shard_map/all_gather | solution.py:33
  14.7 145.9 %reduce-scatter.2.cloned.1.call-start = ((), (), s32[]{:S(2)}) async-start(), calls=%async_computation.2 | async-start | bytes 7372800 | tf_op jit(solution)/shard_map/reduce_scatter | solution.py:37
  88.2 0.8 copy-start.8
  89.5 75.2 %copy-start.6 = (f32[128]{0:T(128)S(1)}, f32[128]{0:T(128)}, u32[]{:S(2)}) copy-start(f32[128]{0:T(128)} %param.14) | copy-start | bytes 1540
  89.6 75.2 %copy-start.7 = (f32[128]{0:T(128)S(1)}, f32[128]{0:T(128)}, u32[]{:S(2)}) copy-start(f32[128]{0:T(128)} %param.13) | copy-start | bytes 1540
  89.6 77.0 %copy-start.3 = (bf16[128,128]{1,0:T(8,128)(2,1)S(1)}, bf16[128,128]{1,0:T(8,128)(2,1)}, u32[]{:S(2)}) copy-start(bf16[128,128]{1,0:T(8,128)(2,1)} %param.15) | copy-start | bytes 98308
  160.6 4.2 %copy-start.2 = (bf16[40,80,128]{2,1,0:T(8,128)(2,1)S(1)}, bf16[40,80,128]{2,1,0:T(8,128)(2,1)}, u32[]{:S(2)}) copy-start(bf16[40,80,128]{2,1,0:T(8,128)(2,1)} %reduce-scatter.2.cloned.1.call-done) | copy-start | bytes 2457604
Sparse Core Ops, SparseCore 0:
  14.8 47.6 all-gather.1
  88.4 72.1 reduce-scatter.1
where the time goes:
time: 175 us
  waiting for transfers between devices  117 us (67%)
  local copies, waits for them, and re-layouts  21.9 us (13%)
  between operations  13.6 us (8%)
  other arithmetic  11.7 us (7%)
  matrix products  10.2 us (6%)
    reduce_scatter x1, waiting for transfers between devices, local(): lax.psum_scatter(jnp.transpose(product, (1, 2, 0)).astype(jnp.bfloat16),...  71 us
    all_gather x1, waiting for transfers between devices, local(): a_rows = lax.all_gather(a_tile, 'rj', axis=1, tiled=True)  46.1 us
    convert_element_type x1, local copies, waits for them, and re-layouts, local(): jnp.transpose(product, (1, 2, 0)).astype(jnp.bfloat16)  11.5 us
    dot_general x1, matrix products, local(): lax.dot_general(a_rows, b_tile, (((0,), (0,)), ((2,), (2,))), preferred_e...  7.43 us
    all_gather x1, local copies, waits for them, and re-layouts, local(): a_rows = lax.all_gather(a_tile, 'rj', axis=1, tiled=True)  6.75 us
    reduce_sum x2, other arithmetic, layer_norm(): var = jnp.mean(centered * centered, axis=-1, keepdims=True)  4.67 us
  transfers between devices with their start and end apart: 2, of which 2 were waited for; matrix products, arithmetic and copies ran while one was open for 1% of the time, Pallas kernels for 0%

commit v1 on v0

--- a/solution.py
+++ b/solution.py
@@ -30,7 +30,12 @@
     gate = jax.nn.sigmoid(jnp.dot(flat, w_gate, preferred_element_type=jnp.float32)).astype(
         jnp.bfloat16
     )
-    a_rows = lax.all_gather(a_tile, "rj", axis=1, tiled=True)
+    ring = [a_tile]
+    for hop in range(3):
+        ring.append(lax.ppermute(ring[-1], "rj", [(dev, (dev + 1) % 4) for dev in range(4)]))
+    a_rows = jnp.roll(
+        jnp.concatenate(ring[::-1], axis=1), (lax.axis_index("rj") + 1) * ring[0].shape[1], axis=1
+    )
     product = lax.dot_general(
         a_rows, b_tile, (((0,), (0,)), ((2,), (2,))), preferred_element_type=jnp.float32
     )

time: 175 us -> 202 us (1.15)
  local copies, waits for them, and re-layouts: 21.9 us -> 39.7 us
  waiting for transfers between devices: 117 us -> 121 us
  starting transfers between devices: 0.08 us -> 3.84 us
    ppermute x0 -> x3, waiting for transfers between devices: none -> 50.1 us  [local(): lax.ppermute(ring[-1], 'rj', [(dev, (dev + 1) % 4) for dev in range(4)])]
    all_gather x1 -> x0, waiting for transfers between devices: 46.1 us -> none  [local(): a_rows = lax.all_gather(a_tile, 'rj', axis=1, tiled=True)]
    concatenate x0 -> x1, local copies, waits for them, and re-layouts: none -> 14 us  [local(): jnp.roll(jnp.concatenate(ring[::-1], axis=1), (lax.axis_index('rj') + 1)...]
    ppermute x0 -> x3, local copies, waits for them, and re-layouts: none -> 7.31 us  [local(): lax.ppermute(ring[-1], 'rj', [(dev, (dev + 1) % 4) for dev in range(4)])]
    all_gather x1 -> x0, local copies, waits for them, and re-layouts: 6.75 us -> none  [local(): a_rows = lax.all_gather(a_tile, 'rj', axis=1, tiled=True)]
    ppermute x0 -> x3, starting transfers between devices: none -> 3.81 us  [local(): lax.ppermute(ring[-1], 'rj', [(dev, (dev + 1) % 4) for dev in range(4)])]
    unnamed x18 -> x24, local copies, waits for them, and re-layouts: 0.77 us -> 2.95 us
  transfers between devices with their start and end apart: 2 -> 4, of which waited for: 2 -> 4; matrix products, arithmetic and copies ran while one was open for 1% -> 5% of each run, Pallas kernels for 0% -> 0%
where the time goes in v1:
time: 202 us; the launch traced here: 201 us
  waiting for transfers between devices  121 us (60%)
  local copies, waits for them, and re-layouts  39.7 us (20%)
  between operations  13.6 us (7%)
  other arithmetic  11.7 us (6%)
  matrix products  11.3 us (6%)
  starting transfers between devices  3.84 us (2%)
    reduce_scatter x1, waiting for transfers between devices, local(): lax.psum_scatter(jnp.transpose(product, (1, 2, 0)).astype(jnp.bfloat16),...  70.6 us
    ppermute x3, waiting for transfers between devices, local(): lax.ppermute(ring[-1], 'rj', [(dev, (dev + 1) % 4) for dev in range(4)])  50.1 us
    concatenate x1, local copies, waits for them, and re-layouts, local(): jnp.roll(jnp.concatenate(ring[::-1], axis=1), (lax.axis_index('rj') + 1)...  14 us
    convert_element_type x1, local copies, waits for them, and re-layouts, local(): jnp.transpose(product, (1, 2, 0)).astype(jnp.bfloat16)  11.5 us
    dot_general x1, matrix products, local(): lax.dot_general(a_rows, b_tile, (((0,), (0,)), ((2,), (2,))), preferred_e...  8.47 us
    ppermute x3, local copies, waits for them, and re-layouts, local(): lax.ppermute(ring[-1], 'rj', [(dev, (dev + 1) % 4) for dev in range(4)])  7.31 us
    reduce_sum x2, other arithmetic, layer_norm(): var = jnp.mean(centered * centered, axis=-1, keepdims=True)  4.67 us
  transfers between devices with their start and end apart: 4, of which 4 were waited for; matrix products, arithmetic and copies ran while one was open for 5% of the time, Pallas kernels for 0%

profile of v1, /device:TPU:0, one launch (start us, length us, event | category | flops | bytes accessed | tf_op | source)
XLA Modules:
  0.0 200.8 jit_solution(8546305763321801935)
XLA Ops:
  6.5 0.0 reduce-scatter.2.cloned.1.call-start
  6.6 1.6 convert_reduce_fusion
  8.2 2.3 %fusion.9 = f32[40,80]{1,0:T(8,128)S(1)} fusion(bf16[40,80,128]{2,1,0:T(8,128)(2,1)} %param.8, f32[40,80]{1,0:T(8,128)S(1)} %broadcast_multiply_fusion.1), kind=kLoop, calls=%fused_computation.14 | loop fusion | flops 1635200 | bytes 844800 | tf_op jit(solution)/shard_map/reduce_sum | solution.py:10
  10.6 1.1 fusion.12
  11.7 0.9 copy-done.3
  12.6 1.0 fusion.26
  13.6 0.9 fusion.17
  14.5 3.0 %collective-permute-start = (bf16[40,80,128]{2,1,0:T(8,128)(2,1)S(1)}, bf16[40,80,128]{2,1,0:T(8,128)(2,1)S(1)}, u32[]{:S(2)}, u32[]{:S(2)}) collective-permute-start(bf16[40,80,128]{2,1,0:T(8,128)(2,1)S(1)} %bitcast.26), channel_id=1, source_target_pairs={{0,1},{1,2},{2,3},{3,0},{4,5},{5,6},{6,7},{7,4},{8,9},{9,10},{10,1... | collective-permute-start | bytes 2457608 | tf_op jit(solution)/shard_map/ppermute | solution.py:35
  17.5 19.2 %collective-permute-done = bf16[40,80,128]{2,1,0:T(8,128)(2,1)S(1)} collective-permute-done((bf16[40,80,128]{2,1,0:T(8,128)(2,1)S(1)}, bf16[40,80,128]{2,1,0:T(8,128)(2,1)S(1)}, u32[]{:S(2)}, u32[]{:S(2)}) %collective-permute-start) | collective-permute-done | bytes 819232 | tf_op jit(solution)/shard_map/ppermute | solution.py:35
  36.7 0.9 copy-done.5
  37.6 0.8 collective-permute-start.1
  38.4 19.6 %collective-permute-done.1 = bf16[40,80,128]{2,1,0:T(8,128)(2,1)} collective-permute-done((bf16[40,80,128]{2,1,0:T(8,128)(2,1)S(1)}, bf16[40,80,128]{2,1,0:T(8,128)(2,1)}, u32[]{:S(2)}, u32[]{:S(2)}) %collective-permute-start.1) | collective-permute-done | bytes 819232 | tf_op jit(solution)/shard_map/ppermute | solution.py:35
  58.0 1.6 copy.41
  59.6 2.2 %copy.46 = bf16[40,80,128]{1,0,2:T(8,128)(2,1)} copy(bf16[40,80,128]{2,1,0:T(8,128)(2,1)S(1)} %bitcast.25) | data formatting | bytes 1638400 | tf_op jit(solution)/shard_map/reshape | solution.py:28
  61.8 2.0 %copy.40 = bf16[40,80,128]{1,0,2:T(8,128)(2,1)S(1)} copy(bf16[40,80,128]{2,1,0:T(8,128)(2,1)} %copy-done.5) | data formatting | bytes 1638400 | tf_op jit(solution)/shard_map/ppermute | solution.py:35
  63.8 2.7 %copy.39 = bf16[40,80,128]{1,0,2:T(8,128)(2,1)} copy(bf16[40,80,128]{2,1,0:T(8,128)(2,1)} %collective-permute-done.1) | data formatting | bytes 1638400 | tf_op jit(solution)/shard_map/ppermute | solution.py:35
  66.5 11.3 %collective-permute-done.2 = bf16[40,80,128]{2,1,0:T(8,128)(2,1)} collective-permute-done((bf16[40,80,128]{2,1,0:T(8,128)(2,1)}, bf16[40,80,128]{2,1,0:T(8,128)(2,1)}, u32[]{:S(2)}, u32[]{:S(2)}) %collective-permute-start.2) | collective-permute-done | bytes 819232 | tf_op jit(solution)/shard_map/ppermute | solution.py:35
  77.8 2.6 %copy.38 = bf16[40,80,128]{1,0,2:T(8,128)(2,1)} copy(bf16[40,80,128]{2,1,0:T(8,128)(2,1)} %collective-permute-done.2) | data formatting | bytes 1638400 | tf_op jit(solution)/shard_map/ppermute | solution.py:35
  80.4 14.0 %concatenate.6 = bf16[40,640,128]{1,0,2:T(8,128)(2,1)} concatenate(bf16[40,80,128]{1,0,2:T(8,128)(2,1)} %copy.38, bf16[40,80,128]{1,0,2:T(8,128)(2,1)} %copy.39, bf16[40,80,128]{1,0,2:T(8,128)(2,1)S(1)} %copy.40, bf16[40,80,128]{1,0,2:T(8,128)(2,1)S(1)} %copy.41, bf16[40,80,128]{1,0,2:T(8,128)(2,1)} %copy.38, bf16[40,80,128]{1,0,2:T(8,128)(2,1)} %copy.39, ...), dimensions={1} | concatenate | bytes 13107200 | tf_op jit(solution)/shard_map/jit(_roll_dynamic)/concatenate | solution.py:36
  94.4 8.5 %convert_bitcast_fusion = bf16[320,80,128]{0,1,2:T(8,128)(2,1)} fusion(bf16[40,80,128]{1,0,2:T(8,128)(2,1)} %copy.46, bf16[40,640,128]{1,0,2:T(8,128)(2,1)} %concatenate.6, s32[]{:T(128)S(6)} %select_n.14), kind=kOutput, calls=%fused_computation | convolution fusion | flops 265420800 | bytes 11796484 | tf_op jit(solution)/shard_map/dot_general | solution.py:39
  102.9 11.5 %copy.47 = bf16[320,80,128]{2,1,0:T(8,128)(2,1)} copy(bf16[320,80,128]{0,1,2:T(8,128)(2,1)} %convert_bitcast_fusion) | data formatting | bytes 13107200 | tf_op jit(solution)/shard_map/convert_element_type | solution.py:43
  114.4 0.0 reduce-scatter.2.cloned.1.call-update
  114.4 1.1 copy-done.4
  115.5 0.6 fusion.4
  116.1 0.0 copy-start.9
  116.2 70.6 %reduce-scatter.2.cloned.1.call-done = bf16[40,80,128]{2,1,0:T(8,128)(2,1)} async-done(((bf16[320,80,128]{2,1,0:T(8,128)(2,1)}), bf16[40,80,128]{2,1,0:T(8,128)(2,1)}) %reduce-scatter.2.cloned.1.call-update) | async-done | bytes 819216 | tf_op jit(solution)/shard_map/reduce_scatter | solution.py:42
  186.7 1.6 convert_reduce_fusion.1
  188.4 0.1 div.29
  188.5 2.3 %multiply_reduce_fusion = f32[40,80]{1,0:T(8,128)S(1)} fusion(f32[40,80]{1,0:T(8,128)S(1)} %broadcast_multiply_fusion, bf16[40,80,128]{2,1,0:T(8,128)(2,1)} %reduce-scatter.2.cloned.1.call-done), kind=kLoop, calls=%fused_computation.35 | loop fusion | flops 1635200 | bytes 844800 | tf_op jit(solution)/shard_map/reduce_sum | solution.py:10
  190.8 0.1 rsqrt.21
  190.9 1.7 fusion.24
  192.7 1.2 fusion.5
  (25 shorter events, 0.1 us)
Async XLA Ops:
  6.5 6.1 %copy-start = (bf16[128,512]{1,0:T(8,128)(2,1)S(1)}, bf16[128,512]{1,0:T(8,128)(2,1)}, u32[]{:S(2)}) copy-start(bf16[128,512]{1,0:T(8,128)(2,1)} %param.11) | copy-start | bytes 393220
  6.5 4.1 %copy-start.1 = (bf16[40,80,128]{2,1,0:T(8,128)(2,1)S(1)}, bf16[40,80,128]{2,1,0:T(8,128)(2,1)}, u32[]{:S(2)}) copy-start(bf16[40,80,128]{2,1,0:T(8,128)(2,1)} %param.8) | copy-start | bytes 2457604
  6.5 4.1 %copy-start.7 = (f32[128]{0:T(128)S(1)}, f32[128]{0:T(128)}, u32[]{:S(2)}) copy-start(f32[128]{0:T(128)} %param.10) | copy-start | bytes 1540
  6.5 4.1 %copy-start.8 = (f32[128]{0:T(128)S(1)}, f32[128]{0:T(128)}, u32[]{:S(2)}) copy-start(f32[128]{0:T(128)} %param.9) | copy-start | bytes 1540
  6.5 180.2 %reduce-scatter.2.cloned.1.call-start = ((), (), s32[]{:S(2)}) async-start(), calls=%async_computation.1 | async-start | bytes 7372800 | tf_op jit(solution)/shard_map/reduce_scatter | solution.py:42
  11.7 0.9 copy-start.3
  14.5 22.2 %collective-permute-start = (bf16[40,80,128]{2,1,0:T(8,128)(2,1)S(1)}, bf16[40,80,128]{2,1,0:T(8,128)(2,1)S(1)}, u32[]{:S(2)}, u32[]{:S(2)}) collective-permute-start(bf16[40,80,128]{2,1,0:T(8,128)(2,1)S(1)} %bitcast.26), channel_id=1, source_target_pairs={{0,1},{1,2},{2,3},{3,0},{4,5},{5,6},{6,7},{7,4},{8,9},{9,10},{10,1... | collective-permute-start | bytes 2457608 | tf_op jit(solution)/shard_map/ppermute | solution.py:35
  36.7 0.9 copy-start.5
  37.6 20.4 %collective-permute-start.1 = (bf16[40,80,128]{2,1,0:T(8,128)(2,1)S(1)}, bf16[40,80,128]{2,1,0:T(8,128)(2,1)}, u32[]{:S(2)}, u32[]{:S(2)}) collective-permute-start(bf16[40,80,128]{2,1,0:T(8,128)(2,1)S(1)} %collective-permute-done), channel_id=1, source_target_pairs={{0,1},{1,2},{2,3},{3,0},{4,5},{5,6},{6,7},{7,4},{8,9},{9,10},{10,1... | collective-permute-start | bytes 2457608 | tf_op jit(solution)/shard_map/ppermute | solution.py:35
  58.0 19.8 %collective-permute-start.2 = (bf16[40,80,128]{2,1,0:T(8,128)(2,1)}, bf16[40,80,128]{2,1,0:T(8,128)(2,1)}, u32[]{:S(2)}, u32[]{:S(2)}) collective-permute-start(bf16[40,80,128]{2,1,0:T(8,128)(2,1)} %collective-permute-done.1), channel_id=1, source_target_pairs={{0,1},{1,2},{2,3},{3,0},{4,5},{5,6},{6,7},{7,4},{8,9},{9,10},{10,1... | collective-permute-start | bytes 2457608 | tf_op jit(solution)/shard_map/ppermute | solution.py:35
  114.4 1.1 copy-start.4
  114.4 1.1 copy-start.11
  116.1 74.8 %copy-start.9 = (f32[128]{0:T(128)S(1)}, f32[128]{0:T(128)}, u32[]{:S(2)}) copy-start(f32[128]{0:T(128)} %param.14) | copy-start | bytes 1540
  116.1 74.8 %copy-start.10 = (f32[128]{0:T(128)S(1)}, f32[128]{0:T(128)}, u32[]{:S(2)}) copy-start(f32[128]{0:T(128)} %param.13) | copy-start | bytes 1540
  116.1 76.5 %copy-start.6 = (bf16[128,128]{1,0:T(8,128)(2,1)S(1)}, bf16[128,128]{1,0:T(8,128)(2,1)}, u32[]{:S(2)}) copy-start(bf16[128,128]{1,0:T(8,128)(2,1)} %param.15) | copy-start | bytes 98308
  186.7 4.2 %copy-start.2 = (bf16[40,80,128]{2,1,0:T(8,128)(2,1)S(1)}, bf16[40,80,128]{2,1,0:T(8,128)(2,1)}, u32[]{:S(2)}) copy-start(bf16[40,80,128]{2,1,0:T(8,128)(2,1)} %reduce-scatter.2.cloned.1.call-done) | copy-start | bytes 2457604
Sparse Core Ops, SparseCore 0:
  114.5 72.1 reduce-scatter.1
